TPU v7x, 32 devices: a whole 2x2x4 slice. The times are simulated.
32 devices in a mesh: dp: 16 (over z, y, core), tensor: 2 (over x).
Axes of the slice: x: 2, y: 2, z: 4, core: 2. Of those that a mesh axis runs over, the one named last changes fastest.
Arguments:
- tokens: bfloat16 [16384, 768], P(('dp', 'tensor')), may hold values from -6 to 6
- query_weight: bfloat16 [768, 768], P('dp', 'tensor'), may hold values from -0.21875 to 0.21875
- query_bias: float32 [768], replicated, may hold values from -3 to 3
- key_weight: bfloat16 [768, 768], P('dp', 'tensor'), may hold values from -0.21875 to 0.21875
- value_weight: bfloat16 [768, 768], P('dp', 'tensor'), may hold values from -0.21875 to 0.21875
- value_bias: float32 [768], replicated, may hold values from -0.625 to 0.625
- output_weight: bfloat16 [768, 768], P('tensor', 'dp'), may hold values from -1.25 to 1.25
- output_bias: float32 [768], replicated, may hold values from -3 to 3
- first_gain: float32 [768], replicated, may hold values from 0.5 to 1.5
- first_shift: float32 [768], replicated, may hold values from -3 to 3
- inner_weight: bfloat16 [768, 3072], P('dp', 'tensor'), may hold values from -0.21875 to 0.21875
- inner_bias: float32 [3072], replicated, may hold values from -3 to 3
- outer_weight: bfloat16 [3072, 768], P('tensor', 'dp'), may hold values from -0.109375 to 0.109375
- outer_bias: float32 [768], replicated, may hold values from -3 to 3
- second_gain: float32 [768], replicated, may hold values from 0.5 to 1.5
- second_shift: float32 [768], replicated, may hold values from -3 to 3
- segments: int32 [16, 1024], P('dp'), may hold values from 0 to 7, never falling along the last dimension, each value on 1 to 768 neighbouring positions
- valid_length: int32 [16], P('dp'), may hold values from 512 to 1024
- cotangent: bfloat16 [16384, 768], P(('dp', 'tensor')), may hold values from -6 to 6
Outputs:
- layer_output: bfloat16 [16384, 768], P(('dp', 'tensor'))
- input_gradient: float32 [16384, 768], P(('dp', 'tensor'))
- query_weight_gradient: float32 [768, 768], P('dp', 'tensor')
- query_bias_gradient: float32 [768], replicated
- key_weight_gradient: float32 [768, 768], P('dp', 'tensor')
- value_weight_gradient: float32 [768, 768], P('dp', 'tensor')
- value_bias_gradient: float32 [768], replicated
- output_weight_gradient: float32 [768, 768], P('tensor', 'dp')
- output_bias_gradient: float32 [768], replicated
- first_gain_gradient: float32 [768], replicated
- first_shift_gradient: float32 [768], replicated
- inner_weight_gradient: float32 [768, 3072], P('dp', 'tensor')
- inner_bias_gradient: float32 [3072], replicated
- outer_weight_gradient: float32 [3072, 768], P('tensor', 'dp')
- outer_bias_gradient: float32 [768], replicated
- second_gain_gradient: float32 [768], replicated
- second_shift_gradient: float32 [768], replicated
Inputs may be any that keep to these rules, and one draw needn't show every extreme that they name: `segments`: segment numbers never fall along a sequence; a token attends only to tokens of its own document. tokens of a sequence at positions valid_length and beyond are padding: no query attends to them as keys except the token itself.
All inputs are finite; a program needn't handle non-finite values.
Results may differ from a plain program's by a relative error of at most 0.013.
Values may be sent and summed in bfloat16 or wider, within the bound.
No kernel may reach another device: no remote copies, remote signals or barrier semaphores. Data moves between devices by JAX's collectives and lax.ppermute only.
A program may use at most 128 MiB of HBM per device.

v0:
```python
import jax
import jax.numpy as jnp
from jax import lax
from jax.sharding import PartitionSpec as P

HEAD_DIM = 64
norm_epsilon = 1e-12
masked_score = -1e30


def normalize(matrix, gain, shift):
    center = matrix - jnp.mean(matrix, axis=-1, keepdims=True)
    spread = jnp.mean(center * center, axis=-1, keepdims=True)
    return center * lax.rsqrt(spread + norm_epsilon) * gain + shift


def exact_gelu(inner):
    return jax.nn.gelu(inner, approximate=False)


def block_scores(query_block, key_seq, segment_row, valid_count, first_row):
    block_rows = query_block.shape[0]
    length = key_seq.shape[0]
    scores = (
        jnp.einsum("qhd,khd->hqk", query_block, key_seq, preferred_element_type=jnp.float32) * 0.125
    )
    positions = jnp.arange(length, dtype=jnp.int32)
    query_pos = first_row + jnp.arange(block_rows, dtype=jnp.int32)
    query_seg = lax.dynamic_slice_in_dim(segment_row, first_row, block_rows)
    allowed = (query_seg[:, None] == segment_row[None, :]) & (
        (positions[None, :] < valid_count) | (query_pos[:, None] == positions[None, :])
    )
    return jnp.where(allowed[None], scores, masked_score)


def attend_sequence(pieces):
    query_seq, key_seq, value_seq, segment_row, valid_count = pieces
    length = query_seq.shape[0]
    block_rows = min(512, length)

    def one_block(block_index):
        first_row = block_index * block_rows
        query_block = lax.dynamic_slice_in_dim(query_seq, first_row, block_rows)
        masked = block_scores(query_block, key_seq, segment_row, valid_count, first_row)
        largest = jnp.max(masked, axis=-1, keepdims=True)
        totals = jnp.sum(jnp.exp(masked - largest), axis=-1, keepdims=True)
        log_total = largest + jnp.log(totals)
        probs_low = jnp.exp(masked - log_total).astype(jnp.bfloat16)
        context = jnp.einsum(
            "hqk,khd->qhd", probs_low, value_seq, preferred_element_type=jnp.float32
        )
        return (context.astype(jnp.bfloat16), log_total[..., 0])

    contexts, log_totals = lax.map(one_block, jnp.arange(length // block_rows, dtype=jnp.int32))
    return (contexts.reshape(query_seq.shape), log_totals)


def attend_backward(pieces):
    query_seq, key_seq, value_seq, segment_row, valid_count, grad_seq, log_totals = pieces
    length = query_seq.shape[0]
    block_rows = min(512, length)

    def one_block(running, inputs):
        key_grad, value_grad = running
        block_index, log_total = inputs
        first_row = block_index * block_rows
        query_block = lax.dynamic_slice_in_dim(query_seq, first_row, block_rows)
        grad_block = lax.dynamic_slice_in_dim(grad_seq, first_row, block_rows)
        masked = block_scores(query_block, key_seq, segment_row, valid_count, first_row)
        probs = jnp.exp(masked - log_total[..., None])
        probs_low = probs.astype(jnp.bfloat16)
        value_grad = value_grad + jnp.einsum(
            "hqk,qhd->khd", probs_low, grad_block, preferred_element_type=jnp.float32
        )
        d_probs = jnp.einsum(
            "qhd,khd->hqk", grad_block, value_seq, preferred_element_type=jnp.float32
        )
        row_inner = jnp.sum(probs * d_probs, axis=-1, keepdims=True)
        d_scores = (probs * (d_probs - row_inner)).astype(jnp.bfloat16)
        query_grad = (
            jnp.einsum("hqk,khd->qhd", d_scores, key_seq, preferred_element_type=jnp.float32)
            * 0.125
        )
        key_grad = (
            key_grad
            + jnp.einsum("hqk,qhd->khd", d_scores, query_block, preferred_element_type=jnp.float32)
            * 0.125
        )
        return ((key_grad, value_grad), query_grad.astype(jnp.bfloat16))

    empty = jnp.zeros(key_seq.shape, jnp.float32)
    block_ids = jnp.arange(length // block_rows, dtype=jnp.int32)
    (key_grad, value_grad), query_grads = lax.scan(
        one_block, (empty, empty), (block_ids, log_totals)
    )
    return (
        query_grads.reshape(query_seq.shape),
        key_grad.astype(jnp.bfloat16),
        value_grad.astype(jnp.bfloat16),
    )


def place_vector(local_part, whole, shard_index):
    width = local_part.shape[0]
    return lax.dynamic_update_slice_in_dim(
        jnp.zeros((whole,), jnp.float32), local_part, shard_index * width, 0
    )


def on_device(
    tokens,
    query_weight,
    query_bias,
    key_weight,
    value_weight,
    value_bias,
    output_weight,
    output_bias,
    first_gain,
    first_shift,
    inner_weight,
    inner_bias,
    outer_weight,
    outer_bias,
    second_gain,
    second_shift,
    segments,
    valid_length,
    cotangent,
):
    head_cols = query_weight.shape[1]
    hidden_cols = inner_weight.shape[1]
    local_heads = head_cols // HEAD_DIM
    shard_index = lax.axis_index("tensor")
    bias_query = lax.dynamic_slice_in_dim(query_bias, shard_index * head_cols, head_cols)
    bias_value = lax.dynamic_slice_in_dim(value_bias, shard_index * head_cols, head_cols)
    bias_inner = lax.dynamic_slice_in_dim(inner_bias, shard_index * hidden_cols, hidden_cols)
    full_query, full_key, full_value, full_output, full_inner, full_outer = (
        lax.all_gather(query_weight, "dp", axis=0, tiled=True),
        lax.all_gather(key_weight, "dp", axis=0, tiled=True),
        lax.all_gather(value_weight, "dp", axis=0, tiled=True),
        lax.all_gather(output_weight, "dp", axis=1, tiled=True),
        lax.all_gather(inner_weight, "dp", axis=0, tiled=True),
        lax.all_gather(outer_weight, "dp", axis=1, tiled=True),
    )
    group_rows = lax.all_gather(tokens, "tensor", axis=0, tiled=True)
    seq_count = segments.shape[0]
    seq_length = segments.shape[1]
    four_shape = (seq_count, seq_length, local_heads, HEAD_DIM)
    queries = (
        jnp.dot(group_rows, full_query, preferred_element_type=jnp.float32) + bias_query
    ).astype(jnp.bfloat16)
    keys_all = jnp.dot(group_rows, full_key, preferred_element_type=jnp.float32).astype(
        jnp.bfloat16
    )
    values_all = (
        jnp.dot(group_rows, full_value, preferred_element_type=jnp.float32) + bias_value
    ).astype(jnp.bfloat16)
    queries = queries.reshape(four_shape)
    keys_all = keys_all.reshape(four_shape)
    values_all = values_all.reshape(four_shape)
    contexts, log_totals = lax.map(
        attend_sequence, (queries, keys_all, values_all, segments, valid_length)
    )
    context = contexts.reshape(seq_count * seq_length, head_cols)
    partial_attn = jnp.dot(context, full_output, preferred_element_type=jnp.float32)
    attended = lax.psum_scatter(partial_attn, "tensor", scatter_dimension=0, tiled=True)
    first_sum = tokens.astype(jnp.float32) + attended + output_bias
    hidden = normalize(first_sum, first_gain, first_shift)
    ffn_rows = lax.all_gather(hidden.astype(jnp.bfloat16), "tensor", axis=0, tiled=True)
    inner = jnp.dot(ffn_rows, full_inner, preferred_element_type=jnp.float32) + bias_inner
    activated = exact_gelu(inner).astype(jnp.bfloat16)
    partial_ffn = jnp.dot(activated, full_outer, preferred_element_type=jnp.float32)
    outer = lax.psum_scatter(partial_ffn, "tensor", scatter_dimension=0, tiled=True)
    second_sum = hidden + outer + outer_bias
    final = normalize(second_sum, second_gain, second_shift)
    layer_output = final.astype(jnp.bfloat16)
    second_value, second_pull = jax.vjp(normalize, second_sum, second_gain, second_shift)
    d_second, second_gain_grad, second_shift_grad = second_pull(cotangent.astype(jnp.float32))
    outer_bias_grad = jnp.sum(d_second, axis=0)
    d_outer = d_second.astype(jnp.bfloat16)
    held = lax.optimization_barrier(
        (query_weight, key_weight, value_weight, output_weight, inner_weight, outer_weight, d_outer)
    )
    d_outer = held[6]
    back_query, back_key, back_value, back_output, back_inner, back_outer = (
        lax.all_gather(held[0], "dp", axis=0, tiled=True),
        lax.all_gather(held[1], "dp", axis=0, tiled=True),
        lax.all_gather(held[2], "dp", axis=0, tiled=True),
        lax.all_gather(held[3], "dp", axis=1, tiled=True),
        lax.all_gather(held[4], "dp", axis=0, tiled=True),
        lax.all_gather(held[5], "dp", axis=1, tiled=True),
    )
    outer_grad_rows = lax.all_gather(d_outer, "tensor", axis=0, tiled=True)
    outer_weight_grad = jnp.einsum(
        "gf,gd->fd", activated, outer_grad_rows, preferred_element_type=jnp.float32
    )
    d_activated = jnp.einsum(
        "gd,fd->gf", outer_grad_rows, back_outer, preferred_element_type=jnp.float32
    )
    gelu_value, gelu_pull = jax.vjp(exact_gelu, inner)
    d_inner = gelu_pull(d_activated)[0].astype(jnp.bfloat16)
    inner_weight_grad = jnp.einsum(
        "gd,gf->df", ffn_rows, d_inner, preferred_element_type=jnp.float32
    )
    inner_bias_local = jnp.sum(d_inner, axis=0, dtype=jnp.float32)
    partial_hidden = jnp.einsum(
        "gf,df->gd", d_inner, back_inner, preferred_element_type=jnp.float32
    )
    d_hidden = d_second + lax.psum_scatter(
        partial_hidden, "tensor", scatter_dimension=0, tiled=True
    )
    first_value, first_pull = jax.vjp(normalize, first_sum, first_gain, first_shift)
    d_first, first_gain_grad, first_shift_grad = first_pull(d_hidden)
    output_bias_grad = jnp.sum(d_first, axis=0)
    attn_grad_rows = lax.all_gather(d_first.astype(jnp.bfloat16), "tensor", axis=0, tiled=True)
    output_weight_grad = jnp.einsum(
        "gc,gd->cd", context, attn_grad_rows, preferred_element_type=jnp.float32
    )
    d_context = jnp.einsum(
        "gd,cd->gc", attn_grad_rows, back_output, preferred_element_type=jnp.float32
    ).astype(jnp.bfloat16)
    d_queries, d_keys, d_values = lax.map(
        attend_backward,
        (
            queries,
            keys_all,
            values_all,
            segments,
            valid_length,
            d_context.reshape(four_shape),
            log_totals,
        ),
    )
    d_queries = d_queries.reshape(seq_count * seq_length, head_cols)
    d_keys = d_keys.reshape(seq_count * seq_length, head_cols)
    d_values = d_values.reshape(seq_count * seq_length, head_cols)
    query_weight_grad = jnp.einsum(
        "gd,gc->dc", group_rows, d_queries, preferred_element_type=jnp.float32
    )
    key_weight_grad = jnp.einsum(
        "gd,gc->dc", group_rows, d_keys, preferred_element_type=jnp.float32
    )
    value_weight_grad = jnp.einsum(
        "gd,gc->dc", group_rows, d_values, preferred_element_type=jnp.float32
    )
    query_bias_local = jnp.sum(d_queries, axis=0, dtype=jnp.float32)
    value_bias_local = jnp.sum(d_values, axis=0, dtype=jnp.float32)
    partial_input = jnp.einsum(
        "gc,dc->gd", d_queries, back_query, preferred_element_type=jnp.float32
    )
    partial_input = partial_input + jnp.einsum(
        "gc,dc->gd", d_keys, back_key, preferred_element_type=jnp.float32
    )
    partial_input = partial_input + jnp.einsum(
        "gc,dc->gd", d_values, back_value, preferred_element_type=jnp.float32
    )
    input_gradient = d_first + lax.psum_scatter(
        partial_input.astype(jnp.bfloat16), "tensor", scatter_dimension=0, tiled=True
    ).astype(jnp.float32)
    query_shard, key_shard, value_shard, output_shard, inner_shard, outer_shard = (
        lax.psum_scatter(query_weight_grad, "dp", scatter_dimension=0, tiled=True),
        lax.psum_scatter(key_weight_grad, "dp", scatter_dimension=0, tiled=True),
        lax.psum_scatter(value_weight_grad, "dp", scatter_dimension=0, tiled=True),
        lax.psum_scatter(output_weight_grad, "dp", scatter_dimension=1, tiled=True),
        lax.psum_scatter(inner_weight_grad, "dp", scatter_dimension=0, tiled=True),
        lax.psum_scatter(outer_weight_grad, "dp", scatter_dimension=1, tiled=True),
    )
    model_width = query_bias.shape[0]
    hidden_width = inner_bias.shape[0]
    query_bias_full = place_vector(query_bias_local, model_width, shard_index)
    value_bias_full = place_vector(value_bias_local, model_width, shard_index)
    inner_bias_full = place_vector(inner_bias_local, hidden_width, shard_index)
    summed = lax.psum(
        (
            query_bias_full,
            value_bias_full,
            output_bias_grad,
            first_gain_grad,
            first_shift_grad,
            inner_bias_full,
            outer_bias_grad,
            second_gain_grad,
            second_shift_grad,
        ),
        ("dp", "tensor"),
    )
    return (
        layer_output,
        input_gradient,
        query_shard,
        summed[0],
        key_shard,
        value_shard,
        summed[1],
        output_shard,
        summed[2],
        summed[3],
        summed[4],
        inner_shard,
        summed[5],
        outer_shard,
        summed[6],
        summed[7],
        summed[8],
    )


def solution(mesh):
    placed = (
        P(("dp", "tensor"), None),
        P("dp", "tensor"),
        P(),
        P("dp", "tensor"),
        P("dp", "tensor"),
        P(),
        P("tensor", "dp"),
        P(),
        P(),
        P(),
        P("dp", "tensor"),
        P(),
        P("tensor", "dp"),
        P(),
        P(),
        P(),
        P("dp", None),
        P("dp"),
        P(("dp", "tensor"), None),
    )
    return jax.shard_map(
        on_device,
        mesh=mesh,
        in_specs=placed,
        out_specs=(
            P(("dp", "tensor"), None),
            P(("dp", "tensor"), None),
            P("dp", "tensor"),
            P(),
            P("dp", "tensor"),
            P("dp", "tensor"),
            P(),
            P("tensor", "dp"),
            P(),
            P(),
            P(),
            P("dp", "tensor"),
            P(),
            P("tensor", "dp"),
            P(),
            P(),
            P(),
        ),
        check_vma=False,
    )
```

profile of v0, /device:TPU:0, one launch (start us, length us, event | category | flops | bytes accessed | tf_op | source)
XLA Modules:
  0.0 1077.9 jit_solution(17472114728465103642)
XLA Ops:
  10.3 25.1 %all_gather.49 = bf16[768,384]{1,0:T(8,128)(2,1)S(1)} all-gather(bf16[48,384]{1,0:T(8,128)(2,1)} %param.24), channel_id=1, replica_groups=mesh['dp'=16,'tensor'=2] {'dp'}, dimensions={0}, use_global_device_ids=true | all-gather | bytes 626688 | tf_op jit(solution)/shard_map/all_gather | solution.py:139
  54.7 20.7 %all_gather.51 = bf16[768,384]{1,0:T(8,128)(2,1)S(1)} all-gather(bf16[48,384]{1,0:T(8,128)(2,1)} %param.27), channel_id=1, replica_groups=mesh['dp'=16,'tensor'=2] {'dp'}, dimensions={0}, use_global_device_ids=true | all-gather | bytes 626688 | tf_op jit(solution)/shard_map/all_gather | solution.py:141
  75.4 20.7 %all_gather.52 = bf16[384,768]{0,1:T(8,128)(2,1)} all-gather(bf16[384,48]{0,1:T(8,128)(2,1)} %param.29), channel_id=1, replica_groups=mesh['dp'=16,'tensor'=2] {'dp'}, dimensions={1}, use_global_device_ids=true | all-gather | bytes 626688 | tf_op jit(solution)/shard_map/all_gather | solution.py:142
  100.2 34.8 %while.47 = (s32[]{:T(128)}, bf16[2,512,6,64]{1,3,2,0:T(8,128)(2,1)S(1)}, f32[2,6,512]{2,1,0:T(8,128)S(1)}, s32[2]{0:T(128)S(1)}, s32[1024]{0:T(1024)S(1)}, /*in...) while((s32[]{:T(128)}, ...), condition=%wide.region_3.4_spmd, body=%wide.region_0.3_spmd.sunk | while | flops 842201600 | bytes 92672240 | solution.py:54
  140.5 41.1 %reduce-scatter.17.cloned.1.call-done = f32[512,768]{1,0:T(8,128)} async-done(((f32[1024,768]{1,0:T(8,128)}), f32[512,768]{1,0:T(8,128)}) %reduce-scatter.17.cloned.1.call-update) | async-done | bytes 1572880 | tf_op jit(solution)/shard_map/reduce_scatter | solution.py:167
  185.7 26.4 %all-gather.11.cloned.1.call-done = bf16[1024,768]{1,0:T(8,128)(2,1)} async-done(((bf16[512,768]{1,0:T(8,128)(2,1)}), bf16[1024,768]{1,0:T(8,128)(2,1)}) %all-gather.11.cloned.1.call-update) | async-done | bytes 1572880 | tf_op jit(solution)/shard_map/all_gather | solution.py:170
  232.0 24.9 %all-gather.15.cloned.1.call-done = bf16[1536,768]{0,1:T(8,128)(2,1)} async-done(((bf16[1536,48]{0,1:T(8,128)(2,1)}), bf16[1536,768]{0,1:T(8,128)(2,1)}) %all-gather.15.cloned.1.call-update) | async-done | bytes 2359312 | tf_op jit(solution)/shard_map/all_gather | solution.py:144
  263.9 41.9 %reduce-scatter.19.cloned.1.call-done = f32[512,768]{1,0:T(8,128)} async-done(((f32[1024,768]{1,0:T(8,128)}), f32[512,768]{1,0:T(8,128)}) %reduce-scatter.19.cloned.1.call-update) | async-done | bytes 1572880 | tf_op jit(solution)/shard_map/reduce_scatter | solution.py:174
  315.8 25.2 %all-gather.17.cloned.1.call-done = bf16[1024,768]{1,0:T(8,128)(2,1)} async-done(((bf16[512,768]{1,0:T(8,128)(2,1)}), bf16[1024,768]{1,0:T(8,128)(2,1)}) %all-gather.17.cloned.1.call-update) | async-done | bytes 1572880 | tf_op jit(solution)/shard_map/all_gather | solution.py:194
  341.0 45.0 %all-gather.19.cloned.1.call-done = bf16[1536,768]{0,1:T(8,128)(2,1)} async-done(((bf16[1536,48]{0,1:T(8,128)(2,1)}), bf16[1536,768]{0,1:T(8,128)(2,1)}) %all-gather.19.cloned.1.call-update) | async-done | bytes 2359312 | tf_op jit(solution)/shard_map/all_gather | solution.py:192
  398.4 30.9 %all-gather.21.cloned.1.call-done = bf16[768,1536]{1,0:T(8,128)(2,1)} async-done(((bf16[48,1536]{1,0:T(8,128)(2,1)}), bf16[768,1536]{1,0:T(8,128)(2,1)}) %all-gather.21.cloned.1.call-update) | async-done | bytes 2359312 | tf_op jit(solution)/shard_map/all_gather | solution.py:191
  436.2 41.9 %reduce-scatter.21.cloned.1.call-done = f32[512,768]{1,0:T(8,128)} async-done(((f32[1024,768]{1,0:T(8,128)}), f32[512,768]{1,0:T(8,128)}) %reduce-scatter.21.cloned.1.call-update) | async-done | bytes 1572880 | tf_op jit(solution)/shard_map/reduce_scatter | solution.py:210
  485.0 23.1 %all_gather.60 = bf16[384,768]{0,1:T(8,128)(2,1)S(1)} all-gather(bf16[384,48]{0,1:T(8,128)(2,1)S(1)} %copy-done.23), channel_id=1, replica_groups=mesh['dp'=16,'tensor'=2] {'dp'}, dimensions={1}, use_global_device_ids=true | all-gather | bytes 626688 | tf_op jit(solution)/shard_map/all_gather | solution.py:190
  508.1 20.4 %all_gather.61 = bf16[768,384]{1,0:T(8,128)(2,1)} all-gather(bf16[48,384]{1,0:T(8,128)(2,1)S(1)} %copy-done.24), channel_id=1, replica_groups=mesh['dp'=16,'tensor'=2] {'dp'}, dimensions={0}, use_global_device_ids=true | all-gather | bytes 626688 | tf_op jit(solution)/shard_map/all_gather | solution.py:187
  528.6 22.0 %all_gather.62 = bf16[768,384]{1,0:T(8,128)(2,1)} all-gather(bf16[48,384]{1,0:T(8,128)(2,1)S(1)} %copy-done.25), channel_id=1, replica_groups=mesh['dp'=16,'tensor'=2] {'dp'}, dimensions={0}, use_global_device_ids=true | all-gather | bytes 626688 | tf_op jit(solution)/shard_map/all_gather | solution.py:188
  550.5 20.4 %all_gather.63 = bf16[768,384]{1,0:T(8,128)(2,1)} all-gather(bf16[48,384]{1,0:T(8,128)(2,1)S(1)} %copy-done.26), channel_id=1, replica_groups=mesh['dp'=16,'tensor'=2] {'dp'}, dimensions={0}, use_global_device_ids=true | all-gather | bytes 626688 | tf_op jit(solution)/shard_map/all_gather | solution.py:189
  575.1 57.7 %while.48 = (s32[]{:T(128)}, f32[1024,6,64]{0,2,1:T(8,128)S(1)}, f32[1024,6,64]{0,2,1:T(8,128)}, bf16[2,512,6,64]{1,3,2,0:T(8,128)(2,1)}, s32[2]{0:T(128)S(1)}, ...) while((s32[]{:T(128)}, f32[1024,6,64]{0,2,1:T(8,128)S(1)}, ...), condition=%wide.region_17.18_spmd.clone, body=%wide.region_15.17_spmd.clone.sunk | while | flops 2064906752 | bytes 144941456 | solution.py:93
  673.5 39.8 %all-reduce = (f32[768]{0:T(1024)}, f32[768]{0:T(1024)}, f32[768]{0:T(1024)}, f32[768]{0:T(1024)}, f32[768]{0:T(1024)}, /*index=5*/f32[3072]{0:T(1024)}, f32[768]{0:T(1024)}, f32[768]{0:T(1024)}, f32[768]{0:T(1024)}) all-reduce(f32[768]{0:T(1024)S(1)} %dynamic_update_slice.32, ...), channel_id=1, replica_groups=mesh['dp'=16,'tensor'=2] {'dp','tensor'}, use_global_device_ids=true, to_apply=%region_21.22 | all-reduce | flops 9216 | bytes 73728 | tf_op jit(solution)/shard_map/psum | solution.py:274
  715.8 29.6 %reduce-scatter.29.cloned.1.call-done = f32[1536,48]{0,1:T(8,128)} async-done(((f32[1536,768]{0,1:T(8,128)}), f32[1536,48]{0,1:T(8,128)}) %reduce-scatter.29.cloned.1.call-update) | async-done | bytes 294928 | tf_op jit(solution)/shard_map/reduce_scatter | solution.py:267
  745.5 79.0 %reduce-scatter.27.cloned.1.call-done = f32[48,1536]{1,0:T(8,128)} async-done(((f32[768,1536]{1,0:T(8,128)}), f32[48,1536]{1,0:T(8,128)}) %reduce-scatter.27.cloned.1.call-update) | async-done | bytes 294928 | tf_op jit(solution)/shard_map/reduce_scatter | solution.py:266
  824.4 61.6 %reduce-scatter.25.cloned.1.call-done = f32[384,48]{0,1:T(8,128)} async-done(((f32[384,768]{0,1:T(8,128)}), f32[384,48]{0,1:T(8,128)}) %reduce-scatter.25.cloned.1.call-update) | async-done | bytes 73744 | tf_op jit(solution)/shard_map/reduce_scatter | solution.py:265
  886.1 61.4 %reduce-scatter.35.cloned.1.call-done = f32[48,384]{1,0:T(8,128)} async-done(((f32[768,384]{1,0:T(8,128)}), f32[48,384]{1,0:T(8,128)}) %reduce-scatter.35.cloned.1.call-update) | async-done | bytes 73744
  947.4 61.5 %reduce-scatter.31.cloned.1.call-done = f32[48,384]{1,0:T(8,128)} async-done(((f32[768,384]{1,0:T(8,128)}), f32[48,384]{1,0:T(8,128)}) %reduce-scatter.31.cloned.1.call-update) | async-done | bytes 73744
  1008.9 61.2 %reduce-scatter.33.cloned.1.call-done = f32[48,384]{1,0:T(8,128)} async-done(((f32[768,384]{1,0:T(8,128)}), f32[48,384]{1,0:T(8,128)}) %reduce-scatter.33.cloned.1.call-update) | async-done | bytes 73744
  (239 shorter events, 234.1 us)
Async XLA Ops:
  8.0 88.0 %all-gather.9.cloned.1.call-start = ((), (), s32[]{:S(2)}) async-start(), calls=%async_computation.10 | async-start | bytes 2359296 | tf_op jit(solution)/shard_map/all_gather | solution.py:146
  8.8 172.9 %reduce-scatter.17.cloned.1.call-start = ((), (), s32[]{:S(2)}) async-start(), calls=%async_computation.11 | async-start | bytes 4718592 | tf_op jit(solution)/shard_map/reduce_scatter | solution.py:167
  137.0 44.7 %copy-start.13 = (bf16[512,768]{1,0:T(8,128)(2,1)S(1)}, bf16[512,768]{1,0:T(8,128)(2,1)}, u32[]{:S(2)}) copy-start(bf16[512,768]{1,0:T(8,128)(2,1)} %param.23) | copy-start | bytes 2359300
  137.0 44.7 %copy-start.36 = (f32[768]{0:T(1024)S(1)}, f32[768]{0:T(1024)}, u32[]{:S(2)}) copy-start(f32[768]{0:T(1024)} %param.30) | copy-start | bytes 9220
  139.7 46.0 %all-gather.13.cloned.1.call-start = ((), (), s32[]{:S(2)}) async-start(), calls=%async_computation.13 | async-start | bytes 2506752 | tf_op jit(solution)/shard_map/all_gather | solution.py:143
  140.3 71.8 %all-gather.11.cloned.1.call-start = ((), (), s32[]{:S(2)}) async-start(), calls=%async_computation.12 | async-start | bytes 2359296 | tf_op jit(solution)/shard_map/all_gather | solution.py:170
  185.0 72.0 %all-gather.15.cloned.1.call-start = ((), (), s32[]{:S(2)}) async-start(), calls=%async_computation.14 | async-start | bytes 2506752 | tf_op jit(solution)/shard_map/all_gather | solution.py:144
  185.5 120.2 %reduce-scatter.19.cloned.1.call-start = ((), (), s32[]{:S(2)}) async-start(), calls=%async_computation.15 | async-start | bytes 4718592 | tf_op jit(solution)/shard_map/reduce_scatter | solution.py:174
  263.8 44.3 %copy-start.12 = (bf16[512,768]{1,0:T(8,128)(2,1)S(1)}, bf16[512,768]{1,0:T(8,128)(2,1)}, u32[]{:S(2)}) copy-start(bf16[512,768]{1,0:T(8,128)(2,1)} %param.41) | copy-start | bytes 2359300
  263.9 44.3 %copy-start.30 = (f32[768]{0:T(1024)S(1)}, f32[768]{0:T(1024)}, u32[]{:S(2)}) copy-start(f32[768]{0:T(1024)} %param.37) | copy-start | bytes 9220
  263.9 77.1 %all-gather.17.cloned.1.call-start = ((), (), s32[]{:S(2)}) async-start(), calls=%async_computation.16 | async-start | bytes 2359296 | tf_op jit(solution)/shard_map/all_gather | solution.py:194
  313.8 72.1 %all-gather.19.cloned.1.call-start = ((), (), s32[]{:S(2)}) async-start(), calls=%async_computation.17 | async-start | bytes 2506752 | tf_op jit(solution)/shard_map/all_gather | solution.py:192
  314.6 114.7 %all-gather.21.cloned.1.call-start = ((), (), s32[]{:S(2)}) async-start(), calls=%async_computation.18 | async-start | bytes 2506752 | tf_op jit(solution)/shard_map/all_gather | solution.py:191
  315.3 162.8 %reduce-scatter.21.cloned.1.call-start = ((), (), s32[]{:S(2)}) async-start(), calls=%async_computation.19 | async-start | bytes 4718592 | tf_op jit(solution)/shard_map/reduce_scatter | solution.py:210
  436.2 134.8 %all-gather.23.cloned.1.call-start = ((), (), s32[]{:S(2)}) async-start(), calls=%async_computation.20 | async-start | bytes 2359296 | tf_op jit(solution)/shard_map/all_gather | solution.py:216
  482.1 46.5 %copy-start.25 = (bf16[48,384]{1,0:T(8,128)(2,1)S(1)}, bf16[48,384]{1,0:T(8,128)(2,1)}, u32[]{:S(2)}) copy-start(bf16[48,384]{1,0:T(8,128)(2,1)} %param.26) | copy-start | bytes 110596
  482.1 68.4 %copy-start.26 = (bf16[48,384]{1,0:T(8,128)(2,1)S(1)}, bf16[48,384]{1,0:T(8,128)(2,1)}, u32[]{:S(2)}) copy-start(bf16[48,384]{1,0:T(8,128)(2,1)} %param.27) | copy-start | bytes 110596
  484.9 228.4 %reduce-scatter.23.cloned.1.call-start = ((), (), s32[]{:S(2)}) async-start(), calls=%async_computation.21 | async-start | bytes 2359296 | tf_op jit(solution)/shard_map/reduce_scatter | solution.py:258
  641.2 104.2 %reduce-scatter.29.cloned.1.call-start = ((), (), s32[]{:S(2)}) async-start(), calls=%async_computation.24 | async-start | bytes 5013504 | tf_op jit(solution)/shard_map/reduce_scatter | solution.py:267
  648.4 176.0 %reduce-scatter.27.cloned.1.call-start = ((), (), s32[]{:S(2)}) async-start(), calls=%async_computation.23 | async-start | bytes 5013504 | tf_op jit(solution)/shard_map/reduce_scatter | solution.py:266
  655.7 230.4 %reduce-scatter.25.cloned.1.call-start = ((), (), s32[]{:S(2)}) async-start(), calls=%async_computation.22 | async-start | bytes 1253376 | tf_op jit(solution)/shard_map/reduce_scatter | solution.py:265
  660.4 287.1 %reduce-scatter.35.cloned.1.call-start = ((), (), s32[]{:S(2)}) async-start(), calls=%async_computation.27 | async-start | bytes 1253376
  664.1 344.8 %reduce-scatter.31.cloned.1.call-start = ((), (), s32[]{:S(2)}) async-start(), calls=%async_computation.25 | async-start | bytes 1253376
  667.8 402.3 %reduce-scatter.33.cloned.1.call-start = ((), (), s32[]{:S(2)}) async-start(), calls=%async_computation.26 | async-start | bytes 1253376
  (39 other events, 351.9 us)
Sparse Core Ops, SparseCore 0:
  10.4 29.8 all-gather.8
  139.8 41.8 reduce-scatter.16
  264.0 41.7 reduce-scatter.18
  436.3 41.7 reduce-scatter.20
  485.0 27.1 all-gather.22
Sparse Core Ops, SparseCore 1:
  142.5 40.8 all-gather.12
  185.3 26.7 all-gather.10
  214.3 42.6 all-gather.14
  313.9 27.0 all-gather.16
  343.3 42.6 all-gather.18
  388.2 40.9 all-gather.20
  641.3 23.6 reduce-scatter.22
  669.3 76.1 reduce-scatter.28
  749.8 74.6 reduce-scatter.26
  828.7 57.3 reduce-scatter.24
  890.1 57.2 reduce-scatter.34
  951.6 57.2 reduce-scatter.30
  1013.0 57.1 reduce-scatter.32
where the time goes:
time: 1090 us; the launch traced here: 1080 us
  waiting for transfers between devices  635 us (58%)
  blocking collectives  212 us (19%)
  matrix products  147 us (13%)
  other arithmetic  42.9 us (4%)
  local copies, waits for them, and re-layouts  20.5 us (2%)
  between operations  16.7 us (2%)
    unnamed x21, waiting for transfers between devices  187 us
    reduce_scatter x1, waiting for transfers between devices, on_device(): lax.psum_scatter(inner_weight_grad, 'dp', scatter_dimension=0, tiled=True)  79 us
    reduce_scatter x1, waiting for transfers between devices, on_device(): lax.psum_scatter(output_weight_grad, 'dp', scatter_dimension=1, tiled=True)  61.6 us
    all_gather x1, waiting for transfers between devices, on_device(): lax.all_gather(held[5], 'dp', axis=1, tiled=True)  45 us
    reduce_scatter x1, waiting for transfers between devices, on_device(): lax.psum_scatter(partial_hidden, 'tensor', scatter_dimension=0, tiled=True)  41.9 us
    reduce_scatter x1, waiting for transfers between devices, on_device(): lax.psum_scatter(partial_ffn, 'tensor', scatter_dimension=0, tiled=True)  41.9 us
    reduce_scatter x1, waiting for transfers between devices, on_device(): lax.psum_scatter(partial_attn, 'tensor', scatter_dimension=0, tiled=True)  41.1 us
    psum x1, blocking collectives, on_device(): lax.psum((query_bias_full, value_bias_full, output_bias_grad, first_gain_...  39.8 us
  transfers between devices with their start and end apart: 18, of which 14 were waited for; matrix products, arithmetic and copies ran while one was open for 6% of the time, Pallas kernels for 0%

commit v1 on v0

--- a/solution.py
+++ b/solution.py
@@ -6,6 +6,28 @@
 HEAD_DIM = 64
 norm_epsilon = 1e-12
 masked_score = -1e30
+
+
+def in_order(parts, dim):
+    shape = list(parts.shape[1:])
+    shape[dim] *= parts.shape[0]
+    return jnp.moveaxis(parts, 0, dim).reshape(shape)
+
+
+def grow_blocks(x, axis):
+    peers = lax.axis_size(axis)
+    tiles = x[None]
+    for level in range(peers.bit_length() - 1):
+        bit = 1 << level
+        partner_block = lax.ppermute(tiles, axis, [(i, i ^ bit) for i in range(peers)])
+        both = jnp.stack([tiles, partner_block])
+        upper = lax.axis_index(axis) >> level & 1
+        tiles = jnp.where(upper == 0, both, both[::-1]).reshape(-1, *x.shape)
+    return tiles
+
+
+def gather_by_bits(shard, axis, dim):
+    return in_order(grow_blocks(shard, axis), dim)
 
 
 def normalize(matrix, gain, shift):
@@ -136,7 +158,7 @@
     bias_value = lax.dynamic_slice_in_dim(value_bias, shard_index * head_cols, head_cols)
     bias_inner = lax.dynamic_slice_in_dim(inner_bias, shard_index * hidden_cols, hidden_cols)
     full_query, full_key, full_value, full_output, full_inner, full_outer = (
-        lax.all_gather(query_weight, "dp", axis=0, tiled=True),
+        gather_by_bits(query_weight, "dp", 0),
         lax.all_gather(key_weight, "dp", axis=0, tiled=True),
         lax.all_gather(value_weight, "dp", axis=0, tiled=True),
         lax.all_gather(output_weight, "dp", axis=1, tiled=True),

time: 1090 us -> 1080 us (level)
  blocking collectives: 212 us -> 195 us
    all_gather x1 -> x0, blocking collectives: 25.1 us -> none  [on_device(): lax.all_gather(query_weight, 'dp', axis=0, tiled=True)]
  transfers between devices with their start and end apart: 18 -> 22, of which waited for: 14 -> 16; matrix products, arithmetic and copies ran while one was open for 6% -> 6% of each run, Pallas kernels for 0% -> 0%
where the time goes in v1:
time: 1080 us; the launch traced here: 1070 us
  waiting for transfers between devices  637 us (59%)
  blocking collectives  195 us (18%)
  matrix products  146 us (14%)
  other arithmetic  44 us (4%)
  local copies, waits for them, and re-layouts  19.2 us (2%)
  between operations  16.8 us (2%)
    unnamed x21, waiting for transfers between devices  187 us
    reduce_scatter x1, waiting for transfers between devices, on_device(): lax.psum_scatter(inner_weight_grad, 'dp', scatter_dimension=0, tiled=True)  79.1 us
    reduce_scatter x1, waiting for transfers between devices, on_device(): lax.psum_scatter(output_weight_grad, 'dp', scatter_dimension=1, tiled=True)  61.7 us
    all_gather x1, waiting for transfers between devices, on_device(): lax.all_gather(held[5], 'dp', axis=1, tiled=True)  45 us
    reduce_scatter x1, waiting for transfers between devices, on_device(): lax.psum_scatter(partial_hidden, 'tensor', scatter_dimension=0, tiled=True)  41.9 us
    reduce_scatter x1, waiting for transfers between devices, on_device(): lax.psum_scatter(partial_ffn, 'tensor', scatter_dimension=0, tiled=True)  41.9 us
    reduce_scatter x1, waiting for transfers between devices, on_device(): lax.psum_scatter(partial_attn, 'tensor', scatter_dimension=0, tiled=True)  40.2 us
    psum x1, blocking collectives, on_device(): lax.psum((query_bias_full, value_bias_full, output_bias_grad, first_gain_...  39.8 us
  transfers between devices with their start and end apart: 22, of which 16 were waited for; matrix products, arithmetic and copies ran while one was open for 6% of the time, Pallas kernels for 0%

profile of v1, /device:TPU:0, one launch (start us, length us, event | category | flops | bytes accessed | tf_op | source)
XLA Modules:
  0.0 1068.7 jit_solution(13991400669540701747)
XLA Ops:
  18.0 22.4 %all_gather.46 = bf16[768,384]{1,0:T(8,128)(2,1)S(1)} all-gather(bf16[48,384]{1,0:T(8,128)(2,1)} %param.26), channel_id=1, replica_groups=mesh['dp'=16,'tensor'=2] {'dp'}, dimensions={0}, use_global_device_ids=true | all-gather | bytes 626688 | tf_op jit(solution)/shard_map/all_gather | solution.py:162
  40.6 24.9 %all_gather.47 = bf16[768,384]{1,0:T(8,128)(2,1)S(1)} all-gather(bf16[48,384]{1,0:T(8,128)(2,1)S(1)} %copy-done.26), channel_id=1, replica_groups=mesh['dp'=16,'tensor'=2] {'dp'}, dimensions={0}, use_global_device_ids=true | all-gather | bytes 626688 | tf_op jit(solution)/shard_map/all_gather | solution.py:163
  65.6 22.1 %all_gather.48 = bf16[384,768]{0,1:T(8,128)(2,1)} all-gather(bf16[384,48]{0,1:T(8,128)(2,1)S(1)} %copy-done.23), channel_id=1, replica_groups=mesh['dp'=16,'tensor'=2] {'dp'}, dimensions={1}, use_global_device_ids=true | all-gather | bytes 626688 | tf_op jit(solution)/shard_map/all_gather | solution.py:164
  92.0 34.8 %while.47 = (s32[]{:T(128)}, bf16[2,512,6,64]{1,3,2,0:T(8,128)(2,1)S(1)}, f32[2,6,512]{2,1,0:T(8,128)S(1)}, s32[2]{0:T(128)S(1)}, s32[1024]{0:T(1024)S(1)}, /*in...) while((s32[]{:T(128)}, ...), condition=%wide.region_3.4_spmd, body=%wide.region_0.3_spmd.sunk | while | flops 842201600 | bytes 92672240 | solution.py:76
  132.1 40.2 %reduce-scatter.17.cloned.1.call-done = f32[512,768]{1,0:T(8,128)} async-done(((f32[1024,768]{1,0:T(8,128)}), f32[512,768]{1,0:T(8,128)}) %reduce-scatter.17.cloned.1.call-update) | async-done | bytes 1572880 | tf_op jit(solution)/shard_map/reduce_scatter | solution.py:189
  176.3 26.4 %all-gather.11.cloned.1.call-done = bf16[1024,768]{1,0:T(8,128)(2,1)} async-done(((bf16[512,768]{1,0:T(8,128)(2,1)}), bf16[1024,768]{1,0:T(8,128)(2,1)}) %all-gather.11.cloned.1.call-update) | async-done | bytes 1572880 | tf_op jit(solution)/shard_map/all_gather | solution.py:192
  222.6 24.8 %all-gather.15.cloned.1.call-done = bf16[1536,768]{0,1:T(8,128)(2,1)} async-done(((bf16[1536,48]{0,1:T(8,128)(2,1)}), bf16[1536,768]{0,1:T(8,128)(2,1)}) %all-gather.15.cloned.1.call-update) | async-done | bytes 2359312 | tf_op jit(solution)/shard_map/all_gather | solution.py:166
  254.4 41.9 %reduce-scatter.19.cloned.1.call-done = f32[512,768]{1,0:T(8,128)} async-done(((f32[1024,768]{1,0:T(8,128)}), f32[512,768]{1,0:T(8,128)}) %reduce-scatter.19.cloned.1.call-update) | async-done | bytes 1572880 | tf_op jit(solution)/shard_map/reduce_scatter | solution.py:196
  306.2 25.2 %all-gather.17.cloned.1.call-done = bf16[1024,768]{1,0:T(8,128)(2,1)} async-done(((bf16[512,768]{1,0:T(8,128)(2,1)}), bf16[1024,768]{1,0:T(8,128)(2,1)}) %all-gather.17.cloned.1.call-update) | async-done | bytes 1572880 | tf_op jit(solution)/shard_map/all_gather | solution.py:216
  331.5 45.0 %all-gather.19.cloned.1.call-done = bf16[1536,768]{0,1:T(8,128)(2,1)} async-done(((bf16[1536,48]{0,1:T(8,128)(2,1)}), bf16[1536,768]{0,1:T(8,128)(2,1)}) %all-gather.19.cloned.1.call-update) | async-done | bytes 2359312 | tf_op jit(solution)/shard_map/all_gather | solution.py:214
  388.8 30.9 %all-gather.21.cloned.1.call-done = bf16[768,1536]{1,0:T(8,128)(2,1)} async-done(((bf16[48,1536]{1,0:T(8,128)(2,1)}), bf16[768,1536]{1,0:T(8,128)(2,1)}) %all-gather.21.cloned.1.call-update) | async-done | bytes 2359312 | tf_op jit(solution)/shard_map/all_gather | solution.py:213
  426.7 41.9 %reduce-scatter.21.cloned.1.call-done = f32[512,768]{1,0:T(8,128)} async-done(((f32[1024,768]{1,0:T(8,128)}), f32[512,768]{1,0:T(8,128)}) %reduce-scatter.21.cloned.1.call-update) | async-done | bytes 1572880 | tf_op jit(solution)/shard_map/reduce_scatter | solution.py:232
  475.5 23.1 %all_gather.56 = bf16[384,768]{0,1:T(8,128)(2,1)S(1)} all-gather(bf16[384,48]{0,1:T(8,128)(2,1)S(1)} %copy-done.24), channel_id=1, replica_groups=mesh['dp'=16,'tensor'=2] {'dp'}, dimensions={1}, use_global_device_ids=true | all-gather | bytes 626688 | tf_op jit(solution)/shard_map/all_gather | solution.py:212
  498.6 20.4 %all_gather.57 = bf16[768,384]{1,0:T(8,128)(2,1)} all-gather(bf16[48,384]{1,0:T(8,128)(2,1)S(1)} %copy-done.28), channel_id=1, replica_groups=mesh['dp'=16,'tensor'=2] {'dp'}, dimensions={0}, use_global_device_ids=true | all-gather | bytes 626688 | tf_op jit(solution)/shard_map/all_gather | solution.py:209
  519.1 22.0 %all_gather.58 = bf16[768,384]{1,0:T(8,128)(2,1)} all-gather(bf16[48,384]{1,0:T(8,128)(2,1)S(1)} %copy-done.25), channel_id=1, replica_groups=mesh['dp'=16,'tensor'=2] {'dp'}, dimensions={0}, use_global_device_ids=true | all-gather | bytes 626688 | tf_op jit(solution)/shard_map/all_gather | solution.py:210
  541.0 20.4 %all_gather.59 = bf16[768,384]{1,0:T(8,128)(2,1)} all-gather(bf16[48,384]{1,0:T(8,128)(2,1)S(1)} %copy-done.27), channel_id=1, replica_groups=mesh['dp'=16,'tensor'=2] {'dp'}, dimensions={0}, use_global_device_ids=true | all-gather | bytes 626688 | tf_op jit(solution)/shard_map/all_gather | solution.py:211
  565.5 57.7 %while.48 = (s32[]{:T(128)}, f32[1024,6,64]{0,2,1:T(8,128)S(1)}, f32[1024,6,64]{0,2,1:T(8,128)}, bf16[2,512,6,64]{1,3,2,0:T(8,128)(2,1)}, s32[2]{0:T(128)S(1)}, ...) while((s32[]{:T(128)}, f32[1024,6,64]{0,2,1:T(8,128)S(1)}, ...), condition=%wide.region_17.18_spmd.clone, body=%wide.region_15.17_spmd.clone.sunk | while | flops 2064906752 | bytes 144941456 | solution.py:115
  664.0 39.8 %all-reduce = (f32[768]{0:T(1024)}, f32[768]{0:T(1024)}, f32[768]{0:T(1024)}, f32[768]{0:T(1024)}, f32[768]{0:T(1024)}, /*index=5*/f32[3072]{0:T(1024)}, f32[768]{0:T(1024)}, f32[768]{0:T(1024)}, f32[768]{0:T(1024)}) all-reduce(f32[768]{0:T(1024)S(1)} %dynamic_update_slice.32, ...), channel_id=1, replica_groups=mesh['dp'=16,'tensor'=2] {'dp','tensor'}, use_global_device_ids=true, to_apply=%region_21.22 | all-reduce | flops 9216 | bytes 73728 | tf_op jit(solution)/shard_map/psum | solution.py:296
  706.3 29.6 %reduce-scatter.29.cloned.1.call-done = f32[1536,48]{0,1:T(8,128)} async-done(((f32[1536,768]{0,1:T(8,128)}), f32[1536,48]{0,1:T(8,128)}) %reduce-scatter.29.cloned.1.call-update) | async-done | bytes 294928 | tf_op jit(solution)/shard_map/reduce_scatter | solution.py:289
  736.0 79.1 %reduce-scatter.27.cloned.1.call-done = f32[48,1536]{1,0:T(8,128)} async-done(((f32[768,1536]{1,0:T(8,128)}), f32[48,1536]{1,0:T(8,128)}) %reduce-scatter.27.cloned.1.call-update) | async-done | bytes 294928 | tf_op jit(solution)/shard_map/reduce_scatter | solution.py:288
  815.0 61.7 %reduce-scatter.25.cloned.1.call-done = f32[384,48]{0,1:T(8,128)} async-done(((f32[384,768]{0,1:T(8,128)}), f32[384,48]{0,1:T(8,128)}) %reduce-scatter.25.cloned.1.call-update) | async-done | bytes 73744 | tf_op jit(solution)/shard_map/reduce_scatter | solution.py:287
  876.7 61.2 %reduce-scatter.35.cloned.1.call-done = f32[48,384]{1,0:T(8,128)} async-done(((f32[768,384]{1,0:T(8,128)}), f32[48,384]{1,0:T(8,128)}) %reduce-scatter.35.cloned.1.call-update) | async-done | bytes 73744
  937.9 61.6 %reduce-scatter.31.cloned.1.call-done = f32[48,384]{1,0:T(8,128)} async-done(((f32[768,384]{1,0:T(8,128)}), f32[48,384]{1,0:T(8,128)}) %reduce-scatter.31.cloned.1.call-update) | async-done | bytes 73744
  999.5 61.4 %reduce-scatter.33.cloned.1.call-done = f32[48,384]{1,0:T(8,128)} async-done(((f32[768,384]{1,0:T(8,128)}), f32[48,384]{1,0:T(8,128)}) %reduce-scatter.33.cloned.1.call-update) | async-done | bytes 73744
  (262 shorter events, 222.7 us)
Async XLA Ops:
  8.1 57.5 %copy-start.23 = (bf16[384,48]{0,1:T(8,128)(2,1)S(1)}, bf16[384,48]{0,1:T(8,128)(2,1)}, u32[]{:S(2)}) copy-start(bf16[384,48]{0,1:T(8,128)(2,1)} %param.29) | copy-start | bytes 110596
  8.1 79.8 %all-gather.9.cloned.1.call-start = ((), (), s32[]{:S(2)}) async-start(), calls=%async_computation.10 | async-start | bytes 2359296 | tf_op jit(solution)/shard_map/all_gather | solution.py:168
  8.1 1.6 collective-permute-start
  10.6 5.5 collective-permute-start.1
  13.5 158.8 %reduce-scatter.17.cloned.1.call-start = ((), (), s32[]{:S(2)}) async-start(), calls=%async_computation.11 | async-start | bytes 4718592 | tf_op jit(solution)/shard_map/reduce_scatter | solution.py:189
  16.1 24.2 %collective-permute-start.2 = (bf16[4,48,384]{2,1,0:T(8,128)(2,1)S(1)}, bf16[4,48,384]{2,1,0:T(8,128)(2,1)S(1)}, u32[]{:S(2)}, u32[]{:S(2)}) collective-permute-start(bf16[4,48,384]{2,1,0:T(8,128)(2,1)S(1)} %bitcast.157), channel_id=1, source_target_pairs={{0,8},{2,10},{4,12},{6,14},{8,0},{10,2},{12,4},{14,6},{16,24},{18,... | collective-permute-start | bytes 442376 | tf_op jit(solution)/shard_map/ppermute | solution.py:22
  40.5 47.2 %collective-permute-start.3 = (bf16[8,48,384]{2,1,0:T(8,128)(2,1)S(1)}, bf16[8,48,384]{2,1,0:T(8,128)(2,1)S(1)}, u32[]{:S(2)}, u32[]{:S(2)}) collective-permute-start(bf16[8,48,384]{2,1,0:T(8,128)(2,1)S(1)} %bitcast.153), channel_id=1, source_target_pairs={{0,16},{2,18},{4,20},{6,22},{8,24},{10,26},{12,28},{14,30},{16,0},... | collective-permute-start | bytes 884744 | tf_op jit(solution)/shard_map/ppermute | solution.py:22
  131.4 44.8 %all-gather.13.cloned.1.call-start = ((), (), s32[]{:S(2)}) async-start(), calls=%async_computation.13 | async-start | bytes 2506752 | tf_op jit(solution)/shard_map/all_gather | solution.py:165
  132.0 70.7 %all-gather.11.cloned.1.call-start = ((), (), s32[]{:S(2)}) async-start(), calls=%async_computation.12 | async-start | bytes 2359296 | tf_op jit(solution)/shard_map/all_gather | solution.py:192
  175.5 71.9 %all-gather.15.cloned.1.call-start = ((), (), s32[]{:S(2)}) async-start(), calls=%async_computation.14 | async-start | bytes 2506752 | tf_op jit(solution)/shard_map/all_gather | solution.py:166
  176.1 120.1 %reduce-scatter.19.cloned.1.call-start = ((), (), s32[]{:S(2)}) async-start(), calls=%async_computation.15 | async-start | bytes 4718592 | tf_op jit(solution)/shard_map/reduce_scatter | solution.py:196
  254.3 77.1 %all-gather.17.cloned.1.call-start = ((), (), s32[]{:S(2)}) async-start(), calls=%async_computation.16 | async-start | bytes 2359296 | tf_op jit(solution)/shard_map/all_gather | solution.py:216
  304.3 72.1 %all-gather.19.cloned.1.call-start = ((), (), s32[]{:S(2)}) async-start(), calls=%async_computation.17 | async-start | bytes 2506752 | tf_op jit(solution)/shard_map/all_gather | solution.py:214
  305.0 114.7 %all-gather.21.cloned.1.call-start = ((), (), s32[]{:S(2)}) async-start(), calls=%async_computation.18 | async-start | bytes 2506752 | tf_op jit(solution)/shard_map/all_gather | solution.py:213
  305.8 162.8 %reduce-scatter.21.cloned.1.call-start = ((), (), s32[]{:S(2)}) async-start(), calls=%async_computation.19 | async-start | bytes 4718592 | tf_op jit(solution)/shard_map/reduce_scatter | solution.py:232
  426.6 134.8 %all-gather.23.cloned.1.call-start = ((), (), s32[]{:S(2)}) async-start(), calls=%async_computation.20 | async-start | bytes 2359296 | tf_op jit(solution)/shard_map/all_gather | solution.py:238
  472.6 68.5 %copy-start.27 = (bf16[48,384]{1,0:T(8,128)(2,1)S(1)}, bf16[48,384]{1,0:T(8,128)(2,1)}, u32[]{:S(2)}) copy-start(bf16[48,384]{1,0:T(8,128)(2,1)} %param.27) | copy-start | bytes 110596
  475.4 228.5 %reduce-scatter.23.cloned.1.call-start = ((), (), s32[]{:S(2)}) async-start(), calls=%async_computation.21 | async-start | bytes 2359296 | tf_op jit(solution)/shard_map/reduce_scatter | solution.py:280
  631.7 104.2 %reduce-scatter.29.cloned.1.call-start = ((), (), s32[]{:S(2)}) async-start(), calls=%async_computation.24 | async-start | bytes 5013504 | tf_op jit(solution)/shard_map/reduce_scatter | solution.py:289
  639.0 176.1 %reduce-scatter.27.cloned.1.call-start = ((), (), s32[]{:S(2)}) async-start(), calls=%async_computation.23 | async-start | bytes 5013504 | tf_op jit(solution)/shard_map/reduce_scatter | solution.py:288
  646.2 230.5 %reduce-scatter.25.cloned.1.call-start = ((), (), s32[]{:S(2)}) async-start(), calls=%async_computation.22 | async-start | bytes 1253376 | tf_op jit(solution)/shard_map/reduce_scatter | solution.py:287
  650.9 287.1 %reduce-scatter.35.cloned.1.call-start = ((), (), s32[]{:S(2)}) async-start(), calls=%async_computation.27 | async-start | bytes 1253376
  654.6 344.9 %reduce-scatter.31.cloned.1.call-start = ((), (), s32[]{:S(2)}) async-start(), calls=%async_computation.25 | async-start | bytes 1253376
  658.4 402.6 %reduce-scatter.33.cloned.1.call-start = ((), (), s32[]{:S(2)}) async-start(), calls=%async_computation.26 | async-start | bytes 1253376
  (47 other events, 718.9 us)
Sparse Core Ops, SparseCore 0:
  13.6 27.4 all-gather.8
  131.5 40.6 reduce-scatter.16
  254.4 41.7 reduce-scatter.18
  426.7 41.7 reduce-scatter.20
  475.5 27.1 all-gather.22
Sparse Core Ops, SparseCore 1:
  134.2 39.6 all-gather.12
  175.9 26.7 all-gather.10
  204.9 42.5 all-gather.14
  304.4 27.0 all-gather.16
  333.8 42.6 all-gather.18
  378.7 40.9 all-gather.20
  631.8 23.6 reduce-scatter.22
  659.8 76.1 reduce-scatter.28
  740.3 74.7 reduce-scatter.26
  819.2 57.4 reduce-scatter.24
  880.8 57.1 reduce-scatter.34
  942.1 57.3 reduce-scatter.30
  1003.6 57.3 reduce-scatter.32
